TPU v7x, 32 devices: a whole 2x2x4 slice. The times are simulated.
32 devices in a mesh: groups: 2 (over x), seq: 16 (over z, y, core).
Axes of the slice: x: 2, y: 2, z: 4, core: 2. Of those that a mesh axis runs over, the one named last changes fastest.
Arguments:
- enc_input: bfloat16 [8192, 1408], P(('groups', 'seq')), parts along dimension 0, may hold values from -6 to 6
- enc_weight: bfloat16 [2816, 1536], P('seq'), may hold values from -0.109375 to 0.109375
- norm_gain: float32 [1536], replicated, may hold values from 0.5 to 1.5
- q_weight: bfloat16 [1536, 1024], replicated, may hold values from -1 to 1
- kv_weight: bfloat16 [1536, 320], replicated, may hold values from -1 to 1
- out_weight: bfloat16 [1536, 1536], replicated, may hold values from -0.15625 to 0.15625
- dec_weight: float32 [3, 1536], replicated, may hold values from -3 to 3
- track_weight: bfloat16 [192, 1536], P('seq'), may hold values from -0.15625 to 0.15625
- track_grad: bfloat16 [4096, 192], P('groups', 'seq'), parts along dimension 0, may hold values from -6 to 6
- track_index: int32 [384], P('groups'), parts along dimension 0, may hold values from 0 to 191, each once
- track_mask: int32 [384], P('groups'), parts along dimension 0, may hold values 0 or 1
Outputs:
- trunk_out: bfloat16 [4096, 1536], P(('groups', 'seq')), parts along dimension 0
- skip_grad: bfloat16 [4096, 1536], P(('groups', 'seq')), parts along dimension 0
- dec_weight_grad: float32 [6, 1536], P('groups'), parts along dimension 0
There are 2 independent parts, one for each index of `groups`. A program takes and returns all parts, laid end to end along the dimension named above; an argument that names none is the same for every part. Nothing has to cross between parts.
Inputs may be any that keep to these rules, and one draw needn't show every extreme that they name: `track_index`: names every track once.
All inputs are finite; a program needn't handle non-finite values.
Results may differ from a plain program's by a relative error of at most 0.02.
Values may be sent and summed in bfloat16 or wider, within the bound.
No kernel may reach another device: no remote copies, remote signals or barrier semaphores. Data moves between devices by JAX's collectives and lax.ppermute only.
A program may use at most 128 MiB of HBM per device.

v0:
```python
import math
import jax
import jax.numpy as jnp
from jax import lax
from jax.sharding import PartitionSpec as P

HEADS = 8
QK = 128
VDIM = 192
DILATION_SPAN = 8


def with_halo(cells, sides, width):
    for axis, dim in sides:
        count = lax.axis_size(axis)
        ends = count - 1
        head = lax.slice_in_dim(cells, 0, width, axis=dim)
        tail = lax.slice_in_dim(cells, cells.shape[dim] - width, cells.shape[dim], axis=dim)
        cells = jnp.concatenate(
            [
                lax.ppermute(tail, axis, [(i, (i + 1) % count) for i in range(ends)]),
                cells,
                lax.ppermute(head, axis, [((i + 1) % count, i) for i in range(ends)]),
            ],
            axis=dim,
        )
    return cells


def gelu_tanh(values):
    return jax.nn.gelu(values, approximate=True)


def attention(tokens, tok_f, norm_gain, q_weight, kv_weight, out_weight):
    token_rows = tokens.shape[0]
    normed = (
        tok_f * lax.rsqrt(jnp.mean(tok_f * tok_f, axis=-1, keepdims=True) + 1e-06) * norm_gain
    ).astype(jnp.bfloat16)
    query = jnp.dot(normed, q_weight, preferred_element_type=jnp.float32).astype(jnp.bfloat16)
    keyval = jnp.dot(normed, kv_weight, preferred_element_type=jnp.float32).astype(jnp.bfloat16)
    query_rows = query.reshape(token_rows * HEADS, QK)

    def block_update(carry, key_block):
        running_max, running_sum, weighted = carry
        scores = lax.dot_general(
            query_rows,
            key_block[:, :QK],
            (((1,), (1,)), ((), ())),
            preferred_element_type=jnp.float32,
        ) * QK ** (-0.5)
        new_max = jnp.maximum(running_max, jnp.max(scores, axis=1))
        shrink = jnp.exp(running_max - new_max)
        expw = jnp.exp(scores - new_max[:, None])
        running_sum = running_sum * shrink + jnp.sum(expw, axis=1)
        weighted = weighted * shrink[:, None] + jnp.dot(
            expw.astype(jnp.bfloat16), key_block[:, QK:], preferred_element_type=jnp.float32
        )
        return (new_max, running_sum, weighted)

    start_state = (
        jnp.full((token_rows * HEADS,), -1e30, jnp.float32),
        jnp.zeros((token_rows * HEADS,), jnp.float32),
        jnp.zeros((token_rows * HEADS, VDIM), jnp.float32),
    )
    carry = start_state
    piece = lax.all_gather(keyval, "seq", axis=0, tiled=True)
    count = piece.shape[0]

    def step_fn(inner, key_block):
        return (block_update(inner, key_block), 0)

    carry, unused = lax.scan(step_fn, carry, piece.reshape(count // 128, 128, piece.shape[1]))
    running_max, running_sum, weighted = carry
    context = (
        (weighted / running_sum[:, None]).reshape(token_rows, HEADS * VDIM).astype(jnp.bfloat16)
    )
    return (tok_f + jnp.dot(context, out_weight, preferred_element_type=jnp.float32)).astype(
        jnp.bfloat16
    )


def decoder_back(tok_f, dec_weight, track_weight, track_grad, track_index, track_mask):
    token_rows = tok_f.shape[0]
    exchanged = lax.all_to_all(track_grad, "seq", split_axis=0, concat_axis=1, tiled=True)
    masked = exchanged * track_mask.astype(jnp.bfloat16)[None, :]
    every_row = lax.all_gather(track_weight, "seq", axis=0, tiled=True)
    selected = jnp.take(every_row, track_index, axis=0)
    head_f = jnp.dot(masked, selected, preferred_element_type=jnp.float32)
    head_gradient = head_f.astype(jnp.bfloat16)
    padded_input = with_halo(head_gradient, (("seq", 0),), DILATION_SPAN).astype(jnp.float32)
    skip_act, pullback = jax.vjp(gelu_tanh, tok_f)
    convback = jnp.zeros(tok_f.shape, jnp.float32)
    tap_terms = []
    for shift_amount in range(3):
        shifted_rows = padded_input[
            DILATION_SPAN * (2 - shift_amount) : DILATION_SPAN * (2 - shift_amount) + token_rows
        ]
        convback = convback + dec_weight[shift_amount][None, :] * shifted_rows
        tap_terms.append(jnp.sum(skip_act * shifted_rows, axis=0))
    skip_grad = pullback(convback)[0].astype(jnp.bfloat16)
    summed = lax.psum(jnp.stack(tap_terms, axis=0), "seq")
    dec_weight_grad = summed / jnp.float32(math.sqrt(token_rows * lax.axis_size("seq")))
    return (skip_grad, dec_weight_grad)


def shards(
    enc_input,
    enc_weight,
    norm_gain,
    q_weight,
    kv_weight,
    out_weight,
    dec_weight,
    track_weight,
    track_grad,
    track_index,
    track_mask,
):
    token_rows = enc_input.shape[0] // 2
    patches = enc_input.reshape(token_rows, 2 * enc_input.shape[1])
    tok_sum = jnp.dot(
        patches,
        lax.all_gather(enc_weight, "seq", axis=0, tiled=True),
        preferred_element_type=jnp.float32,
    )
    tokens = tok_sum.astype(jnp.bfloat16)
    tok_f = tokens.astype(jnp.float32)
    trunk_out = attention(tokens, tok_f, norm_gain, q_weight, kv_weight, out_weight)
    skip_grad, dec_weight_grad = decoder_back(
        tok_f, dec_weight, track_weight, track_grad, track_index, track_mask
    )
    return (trunk_out, skip_grad, dec_weight_grad)


def solution(mesh):
    return jax.shard_map(
        shards,
        mesh=mesh,
        in_specs=(
            P(("groups", "seq"), None),
            P("seq", None),
            P(),
            P(),
            P(),
            P(),
            P(),
            P("seq", None),
            P("groups", "seq"),
            P("groups"),
            P("groups"),
        ),
        out_specs=(P(("groups", "seq"), None), P(("groups", "seq"), None), P("groups", None)),
        check_vma=False,
    )
```

profile of v0, /device:TPU:0, one launch (start us, length us, event | category | flops | bytes accessed | tf_op | source)
XLA Modules:
  0.0 272.7 jit_solution(8789962556055584525)
XLA Ops:
  7.9 1.1 copy.22
  9.6 7.4 %all-to-all-start = ((bf16[16,128,12]{1,2,0:T(8,128)(2,1)}), bf16[16,128,12]{1,2,0:T(8,128)(2,1)S(1)}, u32[]{:S(2)}, u32[]{:S(2)}) async-start(bf16[16,128,12]{1,2,0:T(8,128)(2,1)} %copy.20), calls=%async_computation | async-start | bytes 131072 | tf_op jit(solution)/shard_map/all_to_all | solution.py:84
  17.1 30.1 %all-gather = bf16[16,12,1536]{2,1,0:T(8,128)(2,1)} all-gather(bf16[1,12,1536]{2,1,0:T(8,128)(2,1)} %bitcast.28), channel_id=1, replica_groups=mesh['groups'=2,'seq'=16] {'seq'}, dimensions={0}, use_global_device_ids=true | all-gather | bytes 626688 | tf_op jit(solution)/shard_map/all_gather | solution.py:86
  47.2 2.0 reshape.51
  51.3 3.6 %gather_fusion = bf16[192,1536]{1,0:T(8,128)(2,1)} fusion(bf16[192,1536]{1,0:T(8,128)(2,1)} %reshape.51, s32[1024]{0:T(1024)S(1)} %pad_clamp_fusion), kind=kCustom, calls=%fused_computation | custom fusion | bytes 1180416 | tf_op jit(solution)/shard_map/jit(_take)/gather | solution.py:87
  55.5 1.5 convolution_convert_fusion.1
  57.7 2.8 %collective-permute-start = (bf16[8,1536]{1,0:T(8,128)(2,1)}, bf16[8,1536]{1,0:T(8,128)(2,1)}, u32[]{:S(2)}, u32[]{:S(2)}) collective-permute-start(bf16[8,1536]{1,0:T(8,128)(2,1)} %get-tuple-element.101), channel_id=1, source_target_pairs={{0,1},{1,2},{2,3},{3,4},{4,5},{5,6},{6,7},{7,8},{8,9},{9,10},{10,1... | collective-permute-start | bytes 73736 | tf_op jit(solution)/shard_map/ppermute | solution.py:21
  60.5 1.3 collective-permute-start.1
  61.7 1.5 slice_reduce_fusion.2
  63.2 2.1 reshape.38
  65.4 1.8 maximum_convert_fusion
  67.2 26.1 %all-gather.4.cloned.1.call-done = bf16[2816,1536]{1,0:T(8,128)(2,1)} async-done(((bf16[176,1536]{1,0:T(8,128)(2,1)}), bf16[2816,1536]{1,0:T(8,128)(2,1)}) %all-gather.4.cloned.1.call-update) | async-done | bytes 8650768 | tf_op jit(solution)/shard_map/all_gather | solution.py:123
  93.3 7.5 %multiply_reduce_fusion.3 = (f32[1536]{0:T(1024)S(1)}, f32[1536]{0:T(1024)S(1)}, f32[1536]{0:T(1024)S(1)}, f32[128]{0:T(128)S(1)}, bf16[128,1536]{1,0:T(8,128)(2,1)}, /*index=5*/f32[128,1536]{1,0:T(8,128)S(1)}) fusion(f32[144,1536]{1,0:T(8,128)} %maximum_convert_fusion, f32[1536]{0:T(1024)S(1)} %get-tuple-element.82, f32[1536]{0:T(1024)} %get-tuple-element.83, ...), kind=kOutput, calls=%fused_computation.34 | convolution fusion | flops 1114172800 | bytes 12947968 | tf_op jit(solution)/shard_map/dot_general | solution.py:121
  101.6 1.1 convolution_convert_fusion.3
  102.8 2.5 convolution_convert_fusion.2
  105.3 1.1 reshape.40
  106.4 59.2 %psum.7 = f32[3,1536]{1,0:T(4,128)S(1)} all-reduce(f32[3,1536]{1,0:T(4,128)S(1)} %pad_maximum_fusion), channel_id=1, replica_groups=mesh['groups'=2,'seq'=16] {'seq'}, use_global_device_ids=true, to_apply=%region_8.9 | all-reduce | flops 4608 | bytes 36864 | tf_op jit(solution)/shard_map/psum | solution.py:101
  166.2 2.6 copy.21
  168.7 89.4 %while.15 = (s32[]{:T(128)}, f32[1024]{0:T(1024)S(1)}, f32[1024]{0:T(1024)S(1)}, f32[1024,192]{0,1:T(8,128)}, bf16[16,128,320]{2,1,0:T(8,128)(2,1)}, /*index=5*/bf16[1024,128]{1,0:T(8,128)(2,1)S(1)}, s32[]{:T(128)}, s32[]{:T(128)}) while((s32[]{:T(128)}, f32[1024]{0:T(1024)S(1)}, f32[1024]{0:T(1024)S(1)}, f32[1024,192]{0,1:T(8,128)}, ...), condition=%wide.region_4.5_spmd.clone, body=%wide.region_1.4_spmd.clone.sunk | while | flops 85267456 | bytes 3735653 | solution.py:72
  169.7 1.0 fusion.40
  170.7 1.1 fusion.41
  171.9 2.2 convolution_add_fusion.3
  175.0 1.0 fusion.40
  176.1 1.1 fusion.41
  177.2 2.5 convolution_add_fusion.3
  180.6 1.0 fusion.40
  181.7 1.1 fusion.41
  182.8 2.5 convolution_add_fusion.3
  186.2 1.0 fusion.40
  187.3 1.1 fusion.41
  188.4 2.5 convolution_add_fusion.3
  191.8 1.0 fusion.40
  192.9 1.1 fusion.41
  194.0 2.5 convolution_add_fusion.3
  197.4 1.0 fusion.40
  198.5 1.1 fusion.41
  199.6 2.5 convolution_add_fusion.3
  203.0 1.0 fusion.40
  204.1 1.1 fusion.41
  205.2 2.5 convolution_add_fusion.3
  208.6 1.0 fusion.40
  209.7 1.1 fusion.41
  210.8 2.5 convolution_add_fusion.3
  214.2 1.0 fusion.40
  215.3 1.1 fusion.41
  216.4 2.5 convolution_add_fusion.3
  219.8 1.0 fusion.40
  220.9 1.1 fusion.41
  222.0 2.5 convolution_add_fusion.3
  226.5 1.1 fusion.41
  227.6 2.5 convolution_add_fusion.3
  232.1 1.1 fusion.41
  233.2 2.5 convolution_add_fusion.3
  237.7 1.1 fusion.41
  238.8 2.5 convolution_add_fusion.3
  243.3 1.1 fusion.41
  244.4 2.5 convolution_add_fusion.3
  248.9 1.1 fusion.41
  250.0 2.5 convolution_add_fusion.3
  254.5 1.1 fusion.41
  255.6 2.5 convolution_add_fusion.3
  258.1 1.2 divide_convert_fusion
  260.3 1.5 convert_element_type.46
  261.8 4.1 %fusion.8 = bf16[128,1536]{1,0:T(8,128)(2,1)} fusion(f32[128,1536]{1,0:T(8,128)} %copy-done.1, bf16[128,1536]{1,0:T(8,128)(2,1)S(1)} %convert_element_type.46, bf16[1536,1536]{1,0:T(8,128)(2,1)} %param.18), kind=kOutput, calls=%fused_computation.19 | convolution fusion | flops 604372992 | bytes 6291456 | tf_op jit(solution)/shard_map/dot_general | solution.py:77
  (104 shorter events, 28.3 us)
Async XLA Ops:
  7.2 95.6 %copy-start = (bf16[1536,1024]{1,0:T(8,128)(2,1)S(1)}, bf16[1536,1024]{1,0:T(8,128)(2,1)}, u32[]{:S(2)}) copy-start(bf16[1536,1024]{1,0:T(8,128)(2,1)} %param.16) | copy-start | bytes 9437188
  7.2 86.1 %all-gather.4.cloned.1.call-start = ((), (), s32[]{:S(2)}) async-start(), calls=%async_computation.1 | async-start | bytes 9191424 | tf_op jit(solution)/shard_map/all_gather | solution.py:123
  9.6 45.3 %all-to-all-start = ((bf16[16,128,12]{1,2,0:T(8,128)(2,1)}), bf16[16,128,12]{1,2,0:T(8,128)(2,1)S(1)}, u32[]{:S(2)}, u32[]{:S(2)}) async-start(bf16[16,128,12]{1,2,0:T(8,128)(2,1)} %copy.20), calls=%async_computation | async-start | bytes 131072 | tf_op jit(solution)/shard_map/all_to_all | solution.py:84
  17.0 149.2 %all-gather.6.cloned.1.call-start = ((), (), s32[]{:S(2)}) async-start(), calls=%async_computation.2 | async-start | bytes 1392640 | tf_op jit(solution)/shard_map/all_gather | solution.py:66
  57.7 7.7 %collective-permute-start = (bf16[8,1536]{1,0:T(8,128)(2,1)}, bf16[8,1536]{1,0:T(8,128)(2,1)}, u32[]{:S(2)}, u32[]{:S(2)}) collective-permute-start(bf16[8,1536]{1,0:T(8,128)(2,1)} %get-tuple-element.101), channel_id=1, source_target_pairs={{0,1},{1,2},{2,3},{3,4},{4,5},{5,6},{6,7},{7,8},{8,9},{9,10},{10,1... | collective-permute-start | bytes 73736 | tf_op jit(solution)/shard_map/ppermute | solution.py:21
  60.5 4.9 %collective-permute-start.1 = (bf16[8,1536]{1,0:T(8,128)(2,1)}, bf16[8,1536]{1,0:T(8,128)(2,1)}, u32[]{:S(2)}, u32[]{:S(2)}) collective-permute-start(bf16[8,1536]{1,0:T(8,128)(2,1)} %get-tuple-element.102), channel_id=1, source_target_pairs={{1,0},{2,1},{3,2},{4,3},{5,4},{6,5},{7,6},{8,7},{9,8},{10,9},{11,1... | collective-permute-start | bytes 73736 | tf_op jit(solution)/shard_map/ppermute | solution.py:23
  93.3 8.3 %copy-start.2 = (bf16[1536,320]{0,1:T(8,128)(2,1)S(1)}, bf16[1536,320]{0,1:T(8,128)(2,1)}, u32[]{:S(2)}) copy-start(bf16[1536,320]{0,1:T(8,128)(2,1)} %param.17) | copy-start | bytes 2949124
  93.3 8.3 %copy-start.3 = (f32[1536]{0:T(1024)S(1)}, f32[1536]{0:T(1024)}, u32[]{:S(2)}) copy-start(f32[1536]{0:T(1024)} %param.15) | copy-start | bytes 18436
  100.7 0.9 copy-start.1
Sparse Core Ops, SparseCore 0:
  10.3 82.9 all-gather.3
  102.9 36.2 all-gather.5
where the time goes:
time: 275 us; the launch traced here: 273 us
  blocking collectives  89.3 us (32%)
  matrix products  72.9 us (27%)
  local copies, waits for them, and re-layouts  33.7 us (12%)
  waiting for transfers between devices  26.8 us (10%)
  other arithmetic  24.2 us (9%)
  between operations  14.2 us (5%)
  starting transfers between devices  11.6 us (4%)
    psum x1, blocking collectives, decoder_back(): summed = lax.psum(jnp.stack(tap_terms, axis=0), 'seq')  59.2 us
    dot_general x16, matrix products, block_update(): jnp.dot(expw.astype(jnp.bfloat16), key_block[:, QK:], preferred_element_t...  39.6 us
    all_gather x1, blocking collectives, decoder_back(): every_row = lax.all_gather(track_weight, 'seq', axis=0, tiled=True)  30.1 us
    all_gather x1, waiting for transfers between devices, shards(): lax.all_gather(enc_weight, 'seq', axis=0, tiled=True)  26.1 us
    reduce_sum x16, other arithmetic, block_update(): running_sum = running_sum * shrink + jnp.sum(expw, axis=1)  18.2 us
    dot_general x16, matrix products, block_update(): lax.dot_general(query_rows, key_block[:, :QK], (((1,), (1,)), ((), ())),...  16.7 us
    squeeze x16, local copies, waits for them, and re-layouts, attention(): lax.scan(step_fn, carry, piece.reshape(count // 128, 128, piece.shape[1]))  14.4 us
    dot_general x1, matrix products, shards(): jnp.dot(patches, lax.all_gather(enc_weight, 'seq', axis=0, tiled=True), p...  7.46 us
  transfers between devices with their start and end apart: 5, of which 1 were waited for; matrix products, arithmetic and copies ran while one was open for 8% of the time, Pallas kernels for 0%

commit v1 on v0

--- a/solution.py
+++ b/solution.py
@@ -83,7 +83,12 @@
     token_rows = tok_f.shape[0]
     exchanged = lax.all_to_all(track_grad, "seq", split_axis=0, concat_axis=1, tiled=True)
     masked = exchanged * track_mask.astype(jnp.bfloat16)[None, :]
-    every_row = lax.all_gather(track_weight, "seq", axis=0, tiled=True)
+    ring = [track_weight]
+    for hop in range(15):
+        ring.append(lax.ppermute(ring[-1], "seq", [(dev, (dev + 1) % 16) for dev in range(16)]))
+    every_row = jnp.roll(
+        jnp.concatenate(ring[::-1], axis=0), (lax.axis_index("seq") + 1) * ring[0].shape[0], axis=0
+    )
     selected = jnp.take(every_row, track_index, axis=0)
     head_f = jnp.dot(masked, selected, preferred_element_type=jnp.float32)
     head_gradient = head_f.astype(jnp.bfloat16)

time: 275 us -> 354 us (1.29)
  waiting for transfers between devices: 26.8 us -> 92.8 us
  local copies, waits for them, and re-layouts: 33.7 us -> 74.9 us
  blocking collectives: 89.3 us -> 59.9 us
    ppermute x0 -> x15, waiting for transfers between devices: none -> 92.1 us  [decoder_back(): lax.ppermute(ring[-1], 'seq', [(dev, (dev + 1) % 16) for dev in range(16)])]
    concatenate x0 -> x1, local copies, waits for them, and re-layouts: none -> 40.5 us  [decoder_back(): jnp.roll(jnp.concatenate(ring[::-1], axis=0), (lax.axis_index('seq') + 1)...]
    all_gather x1 -> x0, blocking collectives: 30.1 us -> none  [decoder_back(): every_row = lax.all_gather(track_weight, 'seq', axis=0, tiled=True)]
    all_gather x1, waiting for transfers between devices: 26.1 us -> 0.01 us  [shards(): lax.all_gather(enc_weight, 'seq', axis=0, tiled=True)]
  transfers between devices with their start and end apart: 5 -> 20, of which waited for: 1 -> 15; matrix products, arithmetic and copies ran while one was open for 8% -> 18% of each run, Pallas kernels for 0% -> 0%
where the time goes in v1:
time: 354 us; the launch traced here: 350 us
  waiting for transfers between devices  92.8 us (26%)
  local copies, waits for them, and re-layouts  74.9 us (21%)
  matrix products  72.4 us (20%)
  blocking collectives  59.9 us (17%)
  other arithmetic  25.8 us (7%)
  between operations  14.2 us (4%)
  starting transfers between devices  9.6 us (3%)
    ppermute x15, waiting for transfers between devices, decoder_back(): lax.ppermute(ring[-1], 'seq', [(dev, (dev + 1) % 16) for dev in range(16)])  92.1 us
    psum x1, blocking collectives, decoder_back(): summed = lax.psum(jnp.stack(tap_terms, axis=0), 'seq')  59.9 us
    concatenate x1, local copies, waits for them, and re-layouts, decoder_back(): jnp.roll(jnp.concatenate(ring[::-1], axis=0), (lax.axis_index('seq') + 1)...  40.5 us
    dot_general x16, matrix products, block_update(): jnp.dot(expw.astype(jnp.bfloat16), key_block[:, QK:], preferred_element_t...  39.4 us
    reduce_sum x16, other arithmetic, block_update(): running_sum = running_sum * shrink + jnp.sum(expw, axis=1)  18.2 us
    dot_general x16, matrix products, block_update(): lax.dot_general(query_rows, key_block[:, :QK], (((1,), (1,)), ((), ())),...  16.4 us
    squeeze x16, local copies, waits for them, and re-layouts, attention(): lax.scan(step_fn, carry, piece.reshape(count // 128, 128, piece.shape[1]))  14.4 us
    dot_general x1, matrix products, shards(): jnp.dot(patches, lax.all_gather(enc_weight, 'seq', axis=0, tiled=True), p...  7.51 us
  transfers between devices with their start and end apart: 20, of which 15 were waited for; matrix products, arithmetic and copies ran while one was open for 18% of the time, Pallas kernels for 0%

profile of v1, /device:TPU:0, one launch (start us, length us, event | category | flops | bytes accessed | tf_op | source)
XLA Modules:
  0.0 349.8 jit_solution(9171019349919172593)
XLA Ops:
  8.4 7.0 %collective-permute-done = bf16[12,1536]{1,0:T(8,128)(2,1)S(1)} collective-permute-done((bf16[12,1536]{1,0:T(8,128)(2,1)}, bf16[12,1536]{1,0:T(8,128)(2,1)S(1)}, u32[]{:S(2)}, u32[]{:S(2)}) %collective-permute-start) | collective-permute-done | bytes 36896 | tf_op jit(solution)/shard_map/ppermute | solution.py:88
  15.4 6.2 %collective-permute-done.1 = bf16[12,1536]{1,0:T(8,128)(2,1)S(1)} collective-permute-done((bf16[12,1536]{1,0:T(8,128)(2,1)S(1)}, bf16[12,1536]{1,0:T(8,128)(2,1)S(1)}, u32[]{:S(2)}, u32[]{:S(2)}) %collective-permute-start.1) | collective-permute-done | bytes 36896 | tf_op jit(solution)/shard_map/ppermute | solution.py:88
  21.6 7.1 %collective-permute-done.2 = bf16[12,1536]{1,0:T(8,128)(2,1)S(1)} collective-permute-done((bf16[12,1536]{1,0:T(8,128)(2,1)S(1)}, bf16[12,1536]{1,0:T(8,128)(2,1)S(1)}, u32[]{:S(2)}, u32[]{:S(2)}) %collective-permute-start.2) | collective-permute-done | bytes 36896 | tf_op jit(solution)/shard_map/ppermute | solution.py:88
  28.7 7.2 %collective-permute-done.3 = bf16[12,1536]{1,0:T(8,128)(2,1)S(1)} collective-permute-done((bf16[12,1536]{1,0:T(8,128)(2,1)S(1)}, bf16[12,1536]{1,0:T(8,128)(2,1)S(1)}, u32[]{:S(2)}, u32[]{:S(2)}) %collective-permute-start.3) | collective-permute-done | bytes 36896 | tf_op jit(solution)/shard_map/ppermute | solution.py:88
  35.9 7.2 %collective-permute-done.4 = bf16[12,1536]{1,0:T(8,128)(2,1)S(1)} collective-permute-done((bf16[12,1536]{1,0:T(8,128)(2,1)S(1)}, bf16[12,1536]{1,0:T(8,128)(2,1)S(1)}, u32[]{:S(2)}, u32[]{:S(2)}) %collective-permute-start.4) | collective-permute-done | bytes 36896 | tf_op jit(solution)/shard_map/ppermute | solution.py:88
  43.2 6.2 %collective-permute-done.5 = bf16[12,1536]{1,0:T(8,128)(2,1)S(1)} collective-permute-done((bf16[12,1536]{1,0:T(8,128)(2,1)S(1)}, bf16[12,1536]{1,0:T(8,128)(2,1)S(1)}, u32[]{:S(2)}, u32[]{:S(2)}) %collective-permute-start.5) | collective-permute-done | bytes 36896 | tf_op jit(solution)/shard_map/ppermute | solution.py:88
  49.4 7.1 %collective-permute-done.6 = bf16[12,1536]{1,0:T(8,128)(2,1)S(1)} collective-permute-done((bf16[12,1536]{1,0:T(8,128)(2,1)S(1)}, bf16[12,1536]{1,0:T(8,128)(2,1)S(1)}, u32[]{:S(2)}, u32[]{:S(2)}) %collective-permute-start.6) | collective-permute-done | bytes 36896 | tf_op jit(solution)/shard_map/ppermute | solution.py:88
  56.5 7.2 %collective-permute-done.7 = bf16[12,1536]{1,0:T(8,128)(2,1)S(1)} collective-permute-done((bf16[12,1536]{1,0:T(8,128)(2,1)S(1)}, bf16[12,1536]{1,0:T(8,128)(2,1)S(1)}, u32[]{:S(2)}, u32[]{:S(2)}) %collective-permute-start.7) | collective-permute-done | bytes 36896 | tf_op jit(solution)/shard_map/ppermute | solution.py:88
  63.8 7.2 %collective-permute-done.8 = bf16[12,1536]{1,0:T(8,128)(2,1)S(1)} collective-permute-done((bf16[12,1536]{1,0:T(8,128)(2,1)S(1)}, bf16[12,1536]{1,0:T(8,128)(2,1)S(1)}, u32[]{:S(2)}, u32[]{:S(2)}) %collective-permute-start.8) | collective-permute-done | bytes 36896 | tf_op jit(solution)/shard_map/ppermute | solution.py:88
  71.0 7.2 %collective-permute-done.9 = bf16[12,1536]{1,0:T(8,128)(2,1)S(1)} collective-permute-done((bf16[12,1536]{1,0:T(8,128)(2,1)S(1)}, bf16[12,1536]{1,0:T(8,128)(2,1)S(1)}, u32[]{:S(2)}, u32[]{:S(2)}) %collective-permute-start.9) | collective-permute-done | bytes 36896 | tf_op jit(solution)/shard_map/ppermute | solution.py:88
  79.1 6.5 %collective-permute-done.10 = bf16[12,1536]{1,0:T(8,128)(2,1)} collective-permute-done((bf16[12,1536]{1,0:T(8,128)(2,1)S(1)}, bf16[12,1536]{1,0:T(8,128)(2,1)}, u32[]{:S(2)}, u32[]{:S(2)}) %collective-permute-start.10) | collective-permute-done | bytes 36896 | tf_op jit(solution)/shard_map/ppermute | solution.py:88
  86.3 5.8 %all-to-all-start = ((bf16[16,128,12]{1,2,0:T(8,128)(2,1)}), bf16[16,128,12]{1,2,0:T(8,128)(2,1)S(1)}, u32[]{:S(2)}, u32[]{:S(2)}) async-start(bf16[16,128,12]{1,2,0:T(8,128)(2,1)} %copy.17), calls=%async_computation | async-start | bytes 131072 | tf_op jit(solution)/shard_map/all_to_all | solution.py:84
  93.4 6.1 %collective-permute-done.12 = bf16[12,1536]{1,0:T(8,128)(2,1)S(1)} collective-permute-done((bf16[12,1536]{1,0:T(8,128)(2,1)}, bf16[12,1536]{1,0:T(8,128)(2,1)S(1)}, u32[]{:S(2)}, u32[]{:S(2)}) %collective-permute-start.12) | collective-permute-done | bytes 36896 | tf_op jit(solution)/shard_map/ppermute | solution.py:88
  100.1 1.3 compare_and_fusion
  101.4 5.0 %collective-permute-done.13 = bf16[12,1536]{1,0:T(8,128)(2,1)} collective-permute-done((bf16[12,1536]{1,0:T(8,128)(2,1)S(1)}, bf16[12,1536]{1,0:T(8,128)(2,1)}, u32[]{:S(2)}, u32[]{:S(2)}) %collective-permute-start.13) | collective-permute-done | bytes 36896 | tf_op jit(solution)/shard_map/ppermute | solution.py:88
  107.0 1.2 convert_element_type.48
  108.9 4.1 %collective-permute-done.14 = bf16[12,1536]{1,0:T(8,128)(2,1)} collective-permute-done((bf16[12,1536]{1,0:T(8,128)(2,1)}, bf16[12,1536]{1,0:T(8,128)(2,1)}, u32[]{:S(2)}, u32[]{:S(2)}) %collective-permute-start.14) | collective-permute-done | bytes 36896 | tf_op jit(solution)/shard_map/ppermute | solution.py:88
  113.0 40.5 %concatenate.9 = bf16[384,1536]{1,0:T(8,128)(2,1)} concatenate(bf16[12,1536]{1,0:T(8,128)(2,1)} %collective-permute-done.14, bf16[12,1536]{1,0:T(8,128)(2,1)} %collective-permute-done.13, bf16[12,1536]{1,0:T(8,128)(2,1)} %copy-done.6, bf16[12,1536]{1,0:T(8,128)(2,1)} %collective-permute-done.11, bf16[12,1536]{1,0:T(8,128)(2,1)} %collective-permute-done.10, ...), dimensions={0} | concatenate | bytes 2359296 | tf_op jit(solution)/shard_map/jit(_roll_dynamic)/concatenate | solution.py:89
  153.5 2.0 constant_dynamic-slice_fusion
  155.5 3.8 %gather_fusion = bf16[192,1536]{1,0:T(8,128)(2,1)} fusion(bf16[192,1536]{1,0:T(8,128)(2,1)} %constant_dynamic-slice_fusion, s32[1024]{0:T(1024)} %pad_clamp_fusion), kind=kCustom, calls=%fused_computation | custom fusion | bytes 1180416 | tf_op jit(solution)/shard_map/jit(_take)/gather | solution.py:92
  159.3 1.5 convolution_convert_fusion.1
  161.4 1.9 collective-permute-start.15
  163.3 1.3 collective-permute-start.16
  164.6 1.5 slice_reduce_fusion.2
  166.1 2.1 reshape.38
  168.2 1.8 maximum_convert_fusion
  170.0 7.5 %multiply_reduce_fusion.3 = (f32[1536]{0:T(1024)S(1)}, f32[1536]{0:T(1024)S(1)}, f32[1536]{0:T(1024)S(1)}, f32[128]{0:T(128)S(1)}, bf16[128,1536]{1,0:T(8,128)(2,1)}, /*index=5*/f32[128,1536]{1,0:T(8,128)S(1)}) fusion(f32[144,1536]{1,0:T(8,128)} %maximum_convert_fusion, f32[1536]{0:T(1024)S(1)} %get-tuple-element.76, f32[1536]{0:T(1024)} %get-tuple-element.77, ...), kind=kOutput, calls=%fused_computation.34 | convolution fusion | flops 1114172800 | bytes 12947968 | tf_op jit(solution)/shard_map/dot_general | solution.py:126
  179.7 2.5 convolution_convert_fusion.2
  183.2 59.9 %psum.7 = f32[3,1536]{1,0:T(4,128)S(1)} all-reduce(f32[3,1536]{1,0:T(4,128)S(1)} %pad_maximum_fusion), channel_id=1, replica_groups=mesh['groups'=2,'seq'=16] {'seq'}, use_global_device_ids=true, to_apply=%region_8.9 | all-reduce | flops 4608 | bytes 36864 | tf_op jit(solution)/shard_map/psum | solution.py:106
  243.8 2.6 copy.18
  246.4 88.8 %while.15 = (s32[]{:T(128)}, f32[1024]{0:T(1024)S(1)}, f32[1024]{0:T(1024)S(1)}, f32[1024,192]{0,1:T(8,128)}, bf16[16,128,320]{2,1,0:T(8,128)(2,1)}, /*index=5*/bf16[1024,128]{1,0:T(8,128)(2,1)S(1)}, s32[]{:T(128)}, s32[]{:T(128)}) while((s32[]{:T(128)}, f32[1024]{0:T(1024)S(1)}, f32[1024]{0:T(1024)S(1)}, f32[1024,192]{0,1:T(8,128)}, ...), condition=%wide.region_4.5_spmd.clone, body=%wide.region_1.4_spmd.clone.sunk | while | flops 85267456 | bytes 3735653 | solution.py:72
  248.3 1.1 fusion.41
  249.4 2.2 convolution_add_fusion.3
  253.6 1.1 fusion.41
  254.8 2.5 convolution_add_fusion.3
  259.2 1.1 fusion.41
  260.3 2.5 convolution_add_fusion.3
  264.7 1.1 fusion.41
  265.9 2.5 convolution_add_fusion.3
  270.3 1.1 fusion.41
  271.5 2.5 convolution_add_fusion.3
  277.0 2.5 convolution_add_fusion.3
  281.4 1.1 fusion.41
  282.6 2.5 convolution_add_fusion.3
  287.0 1.1 fusion.41
  288.2 2.5 convolution_add_fusion.3
  292.6 1.1 fusion.41
  293.7 2.5 convolution_add_fusion.3
  298.1 1.1 fusion.41
  299.3 2.5 convolution_add_fusion.3
  303.7 1.1 fusion.41
  304.9 2.5 convolution_add_fusion.3
  309.3 1.1 fusion.41
  310.4 2.5 convolution_add_fusion.3
  314.8 1.1 fusion.41
  316.0 2.5 convolution_add_fusion.3
  320.4 1.1 fusion.41
  321.6 2.5 convolution_add_fusion.3
  327.1 2.5 convolution_add_fusion.3
  331.5 1.1 fusion.41
  332.7 2.5 convolution_add_fusion.3
  335.2 1.2 divide_convert_fusion
  337.4 1.5 convert_element_type.46
  338.9 4.1 %fusion.8 = bf16[128,1536]{1,0:T(8,128)(2,1)} fusion(f32[128,1536]{1,0:T(8,128)} %copy-done.1, bf16[128,1536]{1,0:T(8,128)(2,1)S(1)} %convert_element_type.46, bf16[1536,1536]{1,0:T(8,128)(2,1)} %param.18), kind=kOutput, calls=%fused_computation.19 | convolution fusion | flops 604372992 | bytes 6291456 | tf_op jit(solution)/shard_map/dot_general | solution.py:77
  (146 shorter events, 44.7 us)
Async XLA Ops:
  7.2 172.5 %copy-start = (bf16[1536,1024]{1,0:T(8,128)(2,1)S(1)}, bf16[1536,1024]{1,0:T(8,128)(2,1)}, u32[]{:S(2)}) copy-start(bf16[1536,1024]{1,0:T(8,128)(2,1)} %param.16) | copy-start | bytes 9437188
  7.2 162.8 %all-gather.3.cloned.1.call-start = ((), (), s32[]{:S(2)}) async-start(), calls=%async_computation.1 | async-start | bytes 9191424 | tf_op jit(solution)/shard_map/all_gather | solution.py:128
  7.9 7.5 %collective-permute-start = (bf16[12,1536]{1,0:T(8,128)(2,1)}, bf16[12,1536]{1,0:T(8,128)(2,1)S(1)}, u32[]{:S(2)}, u32[]{:S(2)}) collective-permute-start(bf16[12,1536]{1,0:T(8,128)(2,1)} %param.20), channel_id=1, source_target_pairs={{0,1},{1,2},{2,3},{3,4},{4,5},{5,6},{6,7},{7,8},{8,9},{9,10},{10,1... | collective-permute-start | bytes 110600 | tf_op jit(solution)/shard_map/ppermute | solution.py:88
  15.4 6.2 %collective-permute-start.1 = (bf16[12,1536]{1,0:T(8,128)(2,1)S(1)}, bf16[12,1536]{1,0:T(8,128)(2,1)S(1)}, u32[]{:S(2)}, u32[]{:S(2)}) collective-permute-start(bf16[12,1536]{1,0:T(8,128)(2,1)S(1)} %collective-permute-done), channel_id=1, source_target_pairs={{0,1},{1,2},{2,3},{3,4},{4,5},{5,6},{6,7},{7,8},{8,9},{9,10},{10,1... | collective-permute-start | bytes 110600 | tf_op jit(solution)/shard_map/ppermute | solution.py:88
  21.6 7.1 %collective-permute-start.2 = (bf16[12,1536]{1,0:T(8,128)(2,1)S(1)}, bf16[12,1536]{1,0:T(8,128)(2,1)S(1)}, u32[]{:S(2)}, u32[]{:S(2)}) collective-permute-start(bf16[12,1536]{1,0:T(8,128)(2,1)S(1)} %collective-permute-done.1), channel_id=1, source_target_pairs={{0,1},{1,2},{2,3},{3,4},{4,5},{5,6},{6,7},{7,8},{8,9},{9,10},{10,1... | collective-permute-start | bytes 110600 | tf_op jit(solution)/shard_map/ppermute | solution.py:88
  28.7 7.2 %collective-permute-start.3 = (bf16[12,1536]{1,0:T(8,128)(2,1)S(1)}, bf16[12,1536]{1,0:T(8,128)(2,1)S(1)}, u32[]{:S(2)}, u32[]{:S(2)}) collective-permute-start(bf16[12,1536]{1,0:T(8,128)(2,1)S(1)} %collective-permute-done.2), channel_id=1, source_target_pairs={{0,1},{1,2},{2,3},{3,4},{4,5},{5,6},{6,7},{7,8},{8,9},{9,10},{10,1... | collective-permute-start | bytes 110600 | tf_op jit(solution)/shard_map/ppermute | solution.py:88
  35.9 7.2 %collective-permute-start.4 = (bf16[12,1536]{1,0:T(8,128)(2,1)S(1)}, bf16[12,1536]{1,0:T(8,128)(2,1)S(1)}, u32[]{:S(2)}, u32[]{:S(2)}) collective-permute-start(bf16[12,1536]{1,0:T(8,128)(2,1)S(1)} %collective-permute-done.3), channel_id=1, source_target_pairs={{0,1},{1,2},{2,3},{3,4},{4,5},{5,6},{6,7},{7,8},{8,9},{9,10},{10,1... | collective-permute-start | bytes 110600 | tf_op jit(solution)/shard_map/ppermute | solution.py:88
  43.2 6.2 %collective-permute-start.5 = (bf16[12,1536]{1,0:T(8,128)(2,1)S(1)}, bf16[12,1536]{1,0:T(8,128)(2,1)S(1)}, u32[]{:S(2)}, u32[]{:S(2)}) collective-permute-start(bf16[12,1536]{1,0:T(8,128)(2,1)S(1)} %collective-permute-done.4), channel_id=1, source_target_pairs={{0,1},{1,2},{2,3},{3,4},{4,5},{5,6},{6,7},{7,8},{8,9},{9,10},{10,1... | collective-permute-start | bytes 110600 | tf_op jit(solution)/shard_map/ppermute | solution.py:88
  49.4 7.1 %collective-permute-start.6 = (bf16[12,1536]{1,0:T(8,128)(2,1)S(1)}, bf16[12,1536]{1,0:T(8,128)(2,1)S(1)}, u32[]{:S(2)}, u32[]{:S(2)}) collective-permute-start(bf16[12,1536]{1,0:T(8,128)(2,1)S(1)} %collective-permute-done.5), channel_id=1, source_target_pairs={{0,1},{1,2},{2,3},{3,4},{4,5},{5,6},{6,7},{7,8},{8,9},{9,10},{10,1... | collective-permute-start | bytes 110600 | tf_op jit(solution)/shard_map/ppermute | solution.py:88
  56.5 7.2 %collective-permute-start.7 = (bf16[12,1536]{1,0:T(8,128)(2,1)S(1)}, bf16[12,1536]{1,0:T(8,128)(2,1)S(1)}, u32[]{:S(2)}, u32[]{:S(2)}) collective-permute-start(bf16[12,1536]{1,0:T(8,128)(2,1)S(1)} %collective-permute-done.6), channel_id=1, source_target_pairs={{0,1},{1,2},{2,3},{3,4},{4,5},{5,6},{6,7},{7,8},{8,9},{9,10},{10,1... | collective-permute-start | bytes 110600 | tf_op jit(solution)/shard_map/ppermute | solution.py:88
  63.8 14.5 %copy-start.3 = (bf16[12,1536]{1,0:T(8,128)(2,1)}, bf16[12,1536]{1,0:T(8,128)(2,1)S(1)}, u32[]{:S(2)}) copy-start(bf16[12,1536]{1,0:T(8,128)(2,1)S(1)} %collective-permute-done.7) | copy-start | bytes 110596
  63.8 7.2 %collective-permute-start.8 = (bf16[12,1536]{1,0:T(8,128)(2,1)S(1)}, bf16[12,1536]{1,0:T(8,128)(2,1)S(1)}, u32[]{:S(2)}, u32[]{:S(2)}) collective-permute-start(bf16[12,1536]{1,0:T(8,128)(2,1)S(1)} %collective-permute-done.7), channel_id=1, source_target_pairs={{0,1},{1,2},{2,3},{3,4},{4,5},{5,6},{6,7},{7,8},{8,9},{9,10},{10,1... | collective-permute-start | bytes 110600 | tf_op jit(solution)/shard_map/ppermute | solution.py:88
  71.0 7.2 %copy-start.4 = (bf16[12,1536]{1,0:T(8,128)(2,1)}, bf16[12,1536]{1,0:T(8,128)(2,1)S(1)}, u32[]{:S(2)}) copy-start(bf16[12,1536]{1,0:T(8,128)(2,1)S(1)} %collective-permute-done.8) | copy-start | bytes 110596
  71.0 7.2 %collective-permute-start.9 = (bf16[12,1536]{1,0:T(8,128)(2,1)S(1)}, bf16[12,1536]{1,0:T(8,128)(2,1)S(1)}, u32[]{:S(2)}, u32[]{:S(2)}) collective-permute-start(bf16[12,1536]{1,0:T(8,128)(2,1)S(1)} %collective-permute-done.8), channel_id=1, source_target_pairs={{0,1},{1,2},{2,3},{3,4},{4,5},{5,6},{6,7},{7,8},{8,9},{9,10},{10,1... | collective-permute-start | bytes 110600 | tf_op jit(solution)/shard_map/ppermute | solution.py:88
  78.2 7.4 %copy-start.5 = (bf16[12,1536]{1,0:T(8,128)(2,1)}, bf16[12,1536]{1,0:T(8,128)(2,1)S(1)}, u32[]{:S(2)}) copy-start(bf16[12,1536]{1,0:T(8,128)(2,1)S(1)} %collective-permute-done.9) | copy-start | bytes 110596
  78.2 7.3 %collective-permute-start.10 = (bf16[12,1536]{1,0:T(8,128)(2,1)S(1)}, bf16[12,1536]{1,0:T(8,128)(2,1)}, u32[]{:S(2)}, u32[]{:S(2)}) collective-permute-start(bf16[12,1536]{1,0:T(8,128)(2,1)S(1)} %collective-permute-done.9), channel_id=1, source_target_pairs={{0,1},{1,2},{2,3},{3,4},{4,5},{5,6},{6,7},{7,8},{8,9},{9,10},{10,1... | collective-permute-start | bytes 110600 | tf_op jit(solution)/shard_map/ppermute | solution.py:88
  85.6 7.1 %collective-permute-start.11 = (bf16[12,1536]{1,0:T(8,128)(2,1)}, bf16[12,1536]{1,0:T(8,128)(2,1)}, u32[]{:S(2)}, u32[]{:S(2)}) collective-permute-start(bf16[12,1536]{1,0:T(8,128)(2,1)} %collective-permute-done.10), channel_id=1, source_target_pairs={{0,1},{1,2},{2,3},{3,4},{4,5},{5,6},{6,7},{7,8},{8,9},{9,10},{10,1... | collective-permute-start | bytes 110600 | tf_op jit(solution)/shard_map/ppermute | solution.py:88
  86.3 22.0 %all-to-all-start = ((bf16[16,128,12]{1,2,0:T(8,128)(2,1)}), bf16[16,128,12]{1,2,0:T(8,128)(2,1)S(1)}, u32[]{:S(2)}, u32[]{:S(2)}) async-start(bf16[16,128,12]{1,2,0:T(8,128)(2,1)} %copy.17), calls=%async_computation | async-start | bytes 131072 | tf_op jit(solution)/shard_map/all_to_all | solution.py:84
  92.1 151.7 %all-gather.5.cloned.1.call-start = ((), (), s32[]{:S(2)}) async-start(), calls=%async_computation.2 | async-start | bytes 1392640 | tf_op jit(solution)/shard_map/all_gather | solution.py:66
  92.7 6.8 %collective-permute-start.12 = (bf16[12,1536]{1,0:T(8,128)(2,1)}, bf16[12,1536]{1,0:T(8,128)(2,1)S(1)}, u32[]{:S(2)}, u32[]{:S(2)}) collective-permute-start(bf16[12,1536]{1,0:T(8,128)(2,1)} %collective-permute-done.11), channel_id=1, source_target_pairs={{0,1},{1,2},{2,3},{3,4},{4,5},{5,6},{6,7},{7,8},{8,9},{9,10},{10,1... | collective-permute-start | bytes 110600 | tf_op jit(solution)/shard_map/ppermute | solution.py:88
  99.5 0.6 copy-start.6
  100.1 6.3 %collective-permute-start.13 = (bf16[12,1536]{1,0:T(8,128)(2,1)S(1)}, bf16[12,1536]{1,0:T(8,128)(2,1)}, u32[]{:S(2)}, u32[]{:S(2)}) collective-permute-start(bf16[12,1536]{1,0:T(8,128)(2,1)S(1)} %collective-permute-done.12), channel_id=1, source_target_pairs={{0,1},{1,2},{2,3},{3,4},{4,5},{5,6},{6,7},{7,8},{8,9},{9,10},{10,1... | collective-permute-start | bytes 110600 | tf_op jit(solution)/shard_map/ppermute | solution.py:88
  106.4 6.5 %collective-permute-start.14 = (bf16[12,1536]{1,0:T(8,128)(2,1)}, bf16[12,1536]{1,0:T(8,128)(2,1)}, u32[]{:S(2)}, u32[]{:S(2)}) collective-permute-start(bf16[12,1536]{1,0:T(8,128)(2,1)} %collective-permute-done.13), channel_id=1, source_target_pairs={{0,1},{1,2},{2,3},{3,4},{4,5},{5,6},{6,7},{7,8},{8,9},{9,10},{10,1... | collective-permute-start | bytes 110600 | tf_op jit(solution)/shard_map/ppermute | solution.py:88
  153.5 5.8 %copy-start.8 = (pred[192]{0:T(512)(128)(4,1)S(1)}, pred[192]{0:T(512)(128)(4,1)}, u32[]{:S(2)}) copy-start(pred[192]{0:T(512)(128)(4,1)} %compare_and_fusion) | copy-start | bytes 580
  153.5 5.8 %copy-start.9 = (bf16[192]{0:T(256)(128)(2,1)S(1)}, bf16[192]{0:T(256)(128)(2,1)}, u32[]{:S(2)}) copy-start(bf16[192]{0:T(256)(128)(2,1)} %convert_element_type.48) | copy-start | bytes 1156
  161.4 6.8 %collective-permute-start.15 = (bf16[8,1536]{1,0:T(8,128)(2,1)}, bf16[8,1536]{1,0:T(8,128)(2,1)}, u32[]{:S(2)}, u32[]{:S(2)}) collective-permute-start(bf16[8,1536]{1,0:T(8,128)(2,1)} %get-tuple-element.95), channel_id=1, source_target_pairs={{0,1},{1,2},{2,3},{3,4},{4,5},{5,6},{6,7},{7,8},{8,9},{9,10},{10,1... | collective-permute-start | bytes 73736 | tf_op jit(solution)/shard_map/ppermute | solution.py:21
  163.3 4.9 %collective-permute-start.16 = (bf16[8,1536]{1,0:T(8,128)(2,1)}, bf16[8,1536]{1,0:T(8,128)(2,1)}, u32[]{:S(2)}, u32[]{:S(2)}) collective-permute-start(bf16[8,1536]{1,0:T(8,128)(2,1)} %get-tuple-element.96), channel_id=1, source_target_pairs={{1,0},{2,1},{3,2},{4,3},{5,4},{6,5},{7,6},{8,7},{9,8},{10,9},{11,1... | collective-permute-start | bytes 73736 | tf_op jit(solution)/shard_map/ppermute | solution.py:23
  170.0 8.4 %copy-start.2 = (bf16[1536,320]{0,1:T(8,128)(2,1)S(1)}, bf16[1536,320]{0,1:T(8,128)(2,1)}, u32[]{:S(2)}) copy-start(bf16[1536,320]{0,1:T(8,128)(2,1)} %param.17) | copy-start | bytes 2949124
  170.0 8.4 %copy-start.7 = (f32[1536]{0:T(1024)S(1)}, f32[1536]{0:T(1024)}, u32[]{:S(2)}) copy-start(f32[1536]{0:T(1024)} %param.15) | copy-start | bytes 18436
  177.5 0.9 copy-start.1
Sparse Core Ops, SparseCore 0:
  10.3 82.9 all-gather.2
  179.7 37.0 all-gather.4
